TPU v7x, 256 devices: a whole 4x4x8 slice. The times are simulated.
256 devices in a mesh: row: 8 (over y, core), col: 8 (over x, z_hi), rep: 4 (over z_lo).
Axes of the slice: x: 4, y: 4, z: 8 (z_hi: 2, z_lo: 4; z = z_hi * 4 + z_lo), core: 2. Of those that a mesh axis runs over, the one named last changes fastest.
Arguments:
- features: float32 [256, 32768], P('rep', ('col', 'row')), may hold values from -6 to 6
- weight: float32 [256, 256], replicated, may hold values from -0.375 to 0.375
- cotangent: float32 [256, 32768], P('rep', ('row', 'col')), may hold values from -6 to 6
- tile_values: float32 [10240, 128, 128], P(('row', 'col')), may hold values from -0.078125 to 0.078125
- tile_row: int32 [10240], P(('row', 'col')), may hold values from 0 to 31
- tile_col: int32 [10240], P(('row', 'col')), may hold values from 0 to 31
- tile_kind: int32 [10240], P(('row', 'col')), may hold values from 0 to 159
- tile_count: int32 [64], P(('row', 'col')), may hold values from 40 to 160, as said below
Outputs:
- output: float32 [256, 32768], P('rep', ('row', 'col'))
- input_grad: float32 [256, 32768], P('rep', ('col', 'row'))
- weight_grad: float32 [256, 256], P('rep')
Inputs may be any that keep to these rules, and one draw needn't show every extreme that they name: `tile_count`: a block's slots at or after its count are not part of the adjacency; some block uses all 160 slots. `tile_row`: slots may repeat a tile position; their tiles add. `tile_kind`: an index into the 160 stored tiles of the same block.
All inputs are finite; a program needn't handle non-finite values.
Results may differ from a plain program's by a relative error of at most 0.0001.
Values sent between devices are 32-bit elements; how exact they have to be, the bound alone decides.
No kernel may reach another device: no remote copies, remote signals or barrier semaphores. Data moves between devices by JAX's collectives and lax.ppermute only.
A program may use at most 128 MiB of HBM per device.

v0:
```python
import jax
import jax.numpy as jnp
from jax import lax
from jax.sharding import PartitionSpec as P


def tile_terms(source, values, from_tile, to_tile, tile_kinds, live_weight, dest_tiles, transposed):
    feat_width = source.shape[0]
    tile_edge = values.shape[1]
    tiled = source.reshape(feat_width, source.shape[1] // tile_edge, tile_edge)
    picked = jnp.take(tiled, from_tile, axis=1)
    chosen = jnp.take(values, tile_kinds, axis=0)
    if transposed:
        products = jnp.einsum("fga,gab->fgb", picked, chosen, precision=lax.Precision.HIGHEST)
    else:
        products = jnp.einsum("fgb,gab->fga", picked, chosen, precision=lax.Precision.HIGHEST)
    onehot = (to_tile[:, None] == jnp.arange(dest_tiles, dtype=jnp.int32)[None, :]).astype(
        jnp.float32
    )
    onehot = onehot * live_weight[:, None]
    spread = jnp.einsum("fgt,gd->fdt", products, onehot, precision=lax.Precision.HIGHEST)
    return spread.reshape(feat_width, dest_tiles * tile_edge)


def aggregate(source, values, from_tile, to_tile, tile_kinds, live_count, dest_tiles, transposed):
    slot_total = tile_kinds.shape[0]
    live_weight = (jnp.arange(slot_total, dtype=jnp.int32) < live_count).astype(jnp.float32)
    return tile_terms(
        source, values, from_tile, to_tile, tile_kinds, live_weight, dest_tiles, transposed
    )


def local(features, weight, cotangent, tile_values, tile_row, tile_col, tile_kind, tile_count):
    n_rowdev = lax.axis_size("row")
    n_coldev = lax.axis_size("col")
    n_repdev = lax.axis_size("rep")
    quarter = weight.shape[0] // n_repdev
    rep_index = lax.axis_index("rep")
    own_rows = lax.dynamic_slice_in_dim(weight, rep_index * quarter, quarter, 0)
    own_cols = lax.dynamic_slice_in_dim(weight, rep_index * quarter, quarter, 1)
    stretch_len = features.shape[1]
    tile_edge = tile_values.shape[1]
    live_count = tile_count[0]
    row_tiles = n_coldev * stretch_len // tile_edge
    col_tiles = n_rowdev * stretch_len // tile_edge
    mixed = lax.psum_scatter(
        lax.dot_general(
            own_rows,
            features,
            (((0,), (0,)), ((), ())),
            precision=lax.Precision.HIGHEST,
            preferred_element_type=jnp.float32,
        ),
        "rep",
        scatter_dimension=0,
        tiled=True,
    )
    column_block = lax.all_gather(mixed, "row", axis=1, tiled=True)
    partial_value = aggregate(
        column_block, tile_values, tile_col, tile_row, tile_kind, live_count, row_tiles, False
    )
    summed = lax.psum_scatter(partial_value, "col", scatter_dimension=1, tiled=True)
    output, pullback = jax.vjp(lambda v: jax.nn.gelu(v, approximate=True), summed)
    (grad_pre,) = pullback(cotangent)
    row_block = lax.all_gather(grad_pre, "col", axis=1, tiled=True)
    partial_back = aggregate(
        row_block, tile_values, tile_row, tile_col, tile_kind, live_count, col_tiles, True
    )
    grad_mixed = lax.psum_scatter(partial_back, "row", scatter_dimension=1, tiled=True)
    input_grad = lax.psum_scatter(
        jnp.dot(
            own_cols,
            grad_mixed,
            preferred_element_type=jnp.float32,
            precision=lax.Precision.HIGHEST,
        ),
        "rep",
        scatter_dimension=0,
        tiled=True,
    )
    weight_part = lax.dot_general(
        features,
        lax.all_gather(grad_mixed, "rep", axis=0, tiled=True),
        (((1,), (1,)), ((), ())),
        precision=lax.Precision.HIGHEST,
        preferred_element_type=jnp.float32,
    )
    node_total = stretch_len * n_rowdev * n_coldev
    weight_grad = lax.psum(weight_part * float(node_total) ** (-0.5), ("row", "col"))
    return (output, input_grad, weight_grad)


def solution(mesh):
    return jax.shard_map(
        local,
        mesh=mesh,
        in_specs=(
            P("rep", ("col", "row")),
            P(),
            P("rep", ("row", "col")),
            P(("row", "col"), None, None),
            P(("row", "col")),
            P(("row", "col")),
            P(("row", "col")),
            P(("row", "col")),
        ),
        out_specs=(P("rep", ("row", "col")), P("rep", ("col", "row")), P("rep", None)),
        check_vma=False,
    )
```

profile of v0, /device:TPU:2, one launch (start us, length us, event | category | flops | bytes accessed | tf_op | source)
XLA Modules:
  0.0 1082.4 jit_solution(2901445615518222513)
XLA Ops:
  7.2 0.0 copy-start
  7.2 0.0 reduce-scatter.5.cloned.1.call-start
  7.2 0.9 copy-done
  8.1 2.3 fusion.39
  10.4 0.0 reduce-scatter.5.cloned.1.call-update
  10.5 0.0 all-gather.3.cloned.1.call-start
  10.5 30.2 %reduce-scatter.5.cloned.1.call-done = f32[64,512]{1,0:T(8,128)} async-done(((f32[256,512]{1,0:T(8,128)}), f32[64,512]{1,0:T(8,128)}) %reduce-scatter.5.cloned.1.call-update) | async-done | bytes 131088 | tf_op jit(solution)/shard_map/reduce_scatter | solution.py:46
  40.7 0.0 all-gather.3.cloned.1.call-update
  40.7 0.0 reduce-scatter.7.cloned.1.call-start
  41.4 0.7 compare_select_fusion.2
  42.1 0.0 copy-start.5
  42.1 14.2 %gather_fusion = f32[160,128,128]{2,1,0:T(8,128)} fusion(f32[160,128,128]{2,1,0:T(8,128)} %param.15, s32[1024]{0:T(1024)S(1)} %pad_clamp_fusion.2), kind=kCustom, calls=%fused_computation.clone | custom fusion | bytes 20972160 | tf_op jit(solution)/shard_map/jit(_take)/gather | solution.py:12
  56.3 0.0 copy-done.3
  56.3 0.0 copy-done.5
  56.3 10.5 all-gather.3.cloned.1.call-done
  66.8 1.3 copy_bitcast_fusion.3
  68.2 3.3 gather_fusion.1
  71.5 24.3 %fusion.20 = f32[64,160,128]{2,0,1:T(8,128)S(1)} fusion(f32[160,64,128]{2,1,0:T(8,128)} %gather_fusion.1, pred[160]{0:T(512)(128)(4,1)S(1)} %get-tuple-element.7, f32[160,128,128]{2,1,0:T(8,128)} %gather_fusion, pred[160]{0:T(512)(128)(4,1)S(1)} %get-tuple-element.8), kind=kOutput, calls=%fused_computation.23 | convolution fusion | flops 2017198080 | bytes 20971840 | tf_op jit(solution)/shard_map/fgb,gab->fga/dot_general | solution.py:16
  95.8 0.0 copy-done.4
  95.8 0.0 copy-start.2
  95.8 5.6 fusion.8
  101.5 1.6 copy.29
  103.0 0.0 reduce-scatter.7.cloned.1.call-update
  103.1 0.0 all-gather.5.cloned.1.call-start
  103.1 87.2 %reduce-scatter.7.cloned.1.call-done = f32[64,512]{1,0:T(8,128)} async-done(((f32[64,4096]{1,0:T(8,128)}), f32[64,512]{1,0:T(8,128)}) %reduce-scatter.7.cloned.1.call-update) | async-done | bytes 131088 | tf_op jit(solution)/shard_map/reduce_scatter | solution.py:62
  190.4 0.0 copy-done.2
  190.4 1.7 fusion.36
  192.1 0.0 all-gather.5.cloned.1.call-update
  192.1 0.0 reduce-scatter.9.cloned.1.call-start
  192.2 59.1 %all-gather.5.cloned.1.call-done = f32[64,4096]{1,0:T(8,128)} async-done(((f32[64,512]{1,0:T(8,128)}), f32[64,4096]{1,0:T(8,128)}) %all-gather.5.cloned.1.call-update) | async-done | bytes 1048592 | tf_op jit(solution)/shard_map/all_gather | solution.py:65
  251.3 1.3 copy_bitcast_fusion.2
  252.7 3.3 gather_fusion.2
  255.9 13.9 %fusion.25 = f32[64,160,128]{2,0,1:T(8,128)S(1)} fusion(f32[160,64,128]{2,1,0:T(8,128)} %gather_fusion.2, pred[160]{0:T(512)(128)(4,1)S(1)} %compare_and_fusion, f32[160,128,128]{2,1,0:T(8,128)} %gather_fusion, pred[160]{0:T(512)(128)(4,1)S(1)} %get-tuple-element.8), kind=kOutput, calls=%fused_computation.24 | convolution fusion | flops 2017198080 | bytes 20971840 | tf_op jit(solution)/shard_map/fga,gab->fgb/dot_general | solution.py:14
  269.8 0.0 copy-start.1
  269.8 5.6 fusion.6
  275.5 1.6 copy.28
  277.1 0.0 reduce-scatter.9.cloned.1.call-update
  277.1 0.0 all-reduce.2.cloned.1.call-start
  277.1 30.8 %reduce-scatter.9.cloned.1.call-done = f32[64,512]{1,0:T(8,128)} async-done(((f32[64,4096]{1,0:T(8,128)}), f32[64,512]{1,0:T(8,128)}) %reduce-scatter.9.cloned.1.call-update) | async-done | bytes 131088 | tf_op jit(solution)/shard_map/reduce_scatter | solution.py:69
  307.9 16.4 %all_gather.11 = f32[256,512]{1,0:T(8,128)S(1)} all-gather(f32[64,512]{1,0:T(8,128)} %reduce-scatter.9.cloned.1.call-done), channel_id=1, replica_groups=mesh['row'=8,'col'=8,'rep'=4] {'rep'}, dimensions={0}, use_global_device_ids=true | all-gather | bytes 655360 | tf_op jit(solution)/shard_map/all_gather | solution.py:83
  324.4 1.2 fusion.30
  325.6 0.0 all-reduce.2.cloned.1.call-update
  325.6 0.0 reduce-scatter.11.cloned.1.call-start
  325.7 2.3 fusion.37
  328.0 0.0 reduce-scatter.11.cloned.1.call-update
  328.0 722.2 %all-reduce.2.cloned.1.call-done = f32[64,256]{1,0:T(8,128)} async-done(((f32[64,256]{1,0:T(8,128)}), f32[64,256]{1,0:T(8,128)}) %all-reduce.2.cloned.1.call-update) | async-done | bytes 65552 | tf_op jit(solution)/shard_map/psum | solution.py:89
  1050.2 23.9 %reduce-scatter.11.cloned.1.call-done = f32[64,512]{1,0:T(8,128)} async-done(((f32[256,512]{1,0:T(8,128)}), f32[64,512]{1,0:T(8,128)}) %reduce-scatter.11.cloned.1.call-update) | async-done | bytes 131088 | tf_op jit(solution)/shard_map/reduce_scatter | solution.py:70
  1074.1 1.5 copy.32
  (11 shorter events, 0.1 us)
Async XLA Ops:
  7.2 1.0 copy-start
  7.2 33.5 %reduce-scatter.5.cloned.1.call-start = ((), (), s32[]{:S(2)}) async-start(), calls=%async_computation.4 | async-start | bytes 655360 | tf_op jit(solution)/shard_map/reduce_scatter | solution.py:46
  10.5 56.4 %all-gather.3.cloned.1.call-start = ((), (), s32[]{:S(2)}) async-start(), calls=%async_computation.5 | async-start | bytes 1179648 | tf_op jit(solution)/shard_map/all_gather | solution.py:58
  40.7 149.7 %reduce-scatter.7.cloned.1.call-start = ((), (), s32[]{:S(2)}) async-start(), calls=%async_computation.6 | async-start | bytes 1179648 | tf_op jit(solution)/shard_map/reduce_scatter | solution.py:62
  42.1 14.2 %copy-start.3 = (s32[160]{0:T(256)S(1)}, s32[160]{0:T(256)}, u32[]{:S(2)}) copy-start(s32[160]{0:T(256)} %param.17) | copy-start | bytes 1924
  42.1 14.2 %copy-start.5 = (s32[160]{0:T(256)S(1)}, s32[160]{0:T(256)}, u32[]{:S(2)}) copy-start(s32[160]{0:T(256)} %param.18) | copy-start | bytes 1924
  71.5 24.3 %copy-start.4 = (s32[160]{0:T(256)S(1)}, s32[160]{0:T(256)}, u32[]{:S(2)}) copy-start(s32[160]{0:T(256)} %param.16) | copy-start | bytes 1924
  95.8 94.6 %copy-start.2 = (f32[64,512]{1,0:T(8,128)S(1)}, f32[64,512]{1,0:T(8,128)}, u32[]{:S(2)}) copy-start(f32[64,512]{1,0:T(8,128)} %param.14) | copy-start | bytes 393220
  103.1 148.2 %all-gather.5.cloned.1.call-start = ((), (), s32[]{:S(2)}) async-start(), calls=%async_computation.7 | async-start | bytes 1179648 | tf_op jit(solution)/shard_map/all_gather | solution.py:65
  192.1 115.8 %reduce-scatter.9.cloned.1.call-start = ((), (), s32[]{:S(2)}) async-start(), calls=%async_computation.8 | async-start | bytes 1179648 | tf_op jit(solution)/shard_map/reduce_scatter | solution.py:69
  269.8 54.5 %copy-start.1 = (f32[64,512]{1,0:T(8,128)S(1)}, f32[64,512]{1,0:T(8,128)}, u32[]{:S(2)}) copy-start(f32[64,512]{1,0:T(8,128)} %param.12) | copy-start | bytes 393220
  277.1 773.1 %all-reduce.2.cloned.1.call-start = ((), (), s32[]{:S(2)}) async-start(), calls=%async_computation.10 | async-start | bytes 131072 | tf_op jit(solution)/shard_map/psum | solution.py:89
  325.6 748.5 %reduce-scatter.11.cloned.1.call-start = ((), (), s32[]{:S(2)}) async-start(), calls=%async_computation.9 | async-start | bytes 655360 | tf_op jit(solution)/shard_map/reduce_scatter | solution.py:70
Sparse Core Ops, SparseCore 0:
  10.6 30.0 reduce-scatter.4
  42.5 24.2 all-gather.2
  103.2 87.1 reduce-scatter.6
  193.4 57.8 all-gather.4
  277.2 30.6 reduce-scatter.8
  325.7 724.4 all-reduce.1
  1053.3 20.7 reduce-scatter.10
where the time goes:
time: 1080 us
  waiting for transfers between devices  964 us (89%)
  matrix products  55.3 us (5%)
  local copies, waits for them, and re-layouts  29 us (3%)
  blocking collectives  16.4 us (2%)
  between operations  14.9 us (1%)
    psum x1, waiting for transfers between devices, local(): lax.psum(weight_part * float(node_total) ** (-0.5), ('row', 'col'))  722 us
    reduce_scatter x1, waiting for transfers between devices, local(): lax.psum_scatter(partial_value, 'col', scatter_dimension=1, tiled=True)  87.2 us
    all_gather x1, waiting for transfers between devices, local(): row_block = lax.all_gather(grad_pre, 'col', axis=1, tiled=True)  59.1 us
    reduce_scatter x1, waiting for transfers between devices, local(): lax.psum_scatter(partial_back, 'row', scatter_dimension=1, tiled=True)  30.8 us
    reduce_scatter x1, waiting for transfers between devices, local(): lax.psum_scatter(lax.dot_general(own_rows, features, (((0,), (0,)), ((),...  30.2 us
    dot_general x1, matrix products, tile_terms(): jnp.einsum('fgb,gab->fga', picked, chosen, precision=lax.Precision.HIGHEST)  24.3 us
    reduce_scatter x1, waiting for transfers between devices, local(): lax.psum_scatter(jnp.dot(own_cols, grad_mixed, preferred_element_type=jnp...  23.9 us
  transfers between devices with their start and end apart: 7, of which 7 were waited for; matrix products, arithmetic and copies ran while one was open for 2% of the time, Pallas kernels for 0%

commit v1 on v0

--- a/solution.py
+++ b/solution.py
@@ -62,7 +62,9 @@
     summed = lax.psum_scatter(partial_value, "col", scatter_dimension=1, tiled=True)
     output, pullback = jax.vjp(lambda v: jax.nn.gelu(v, approximate=True), summed)
     (grad_pre,) = pullback(cotangent)
-    row_block = lax.all_gather(grad_pre, "col", axis=1, tiled=True)
+    row_block = jnp.concatenate(
+        lax.all_to_all(jnp.stack([grad_pre] * lax.axis_size("col")), "col", 0, 0), axis=1
+    )
     partial_back = aggregate(
         row_block, tile_values, tile_row, tile_col, tile_kind, live_count, col_tiles, True
     )

time: 1080 us -> 1060 us (0.981)
  waiting for transfers between devices: 964 us -> 934 us
    all_gather x1 -> x0, waiting for transfers between devices: 59.1 us -> none  [local(): row_block = lax.all_gather(grad_pre, 'col', axis=1, tiled=True)]
    all_to_all x0 -> x1, waiting for transfers between devices: none -> 27 us  [local(): lax.all_to_all(jnp.stack([grad_pre] * lax.axis_size('col')), 'col', 0, 0)]
where the time goes in v1:
time: 1060 us
  waiting for transfers between devices  934 us (88%)
  matrix products  55.3 us (5%)
  local copies, waits for them, and re-layouts  30 us (3%)
  blocking collectives  16.4 us (2%)
  between operations  14.9 us (1%)
    psum x1, waiting for transfers between devices, local(): lax.psum(weight_part * float(node_total) ** (-0.5), ('row', 'col'))  722 us
    reduce_scatter x1, waiting for transfers between devices, local(): lax.psum_scatter(partial_value, 'col', scatter_dimension=1, tiled=True)  87.3 us
    reduce_scatter x1, waiting for transfers between devices, local(): lax.psum_scatter(partial_back, 'row', scatter_dimension=1, tiled=True)  32.7 us
    reduce_scatter x1, waiting for transfers between devices, local(): lax.psum_scatter(lax.dot_general(own_rows, features, (((0,), (0,)), ((),...  30.2 us
    all_to_all x1, waiting for transfers between devices, local(): lax.all_to_all(jnp.stack([grad_pre] * lax.axis_size('col')), 'col', 0, 0)  27 us
    dot_general x1, matrix products, tile_terms(): jnp.einsum('fgb,gab->fga', picked, chosen, precision=lax.Precision.HIGHEST)  24.3 us
    reduce_scatter x1, waiting for transfers between devices, local(): lax.psum_scatter(jnp.dot(own_cols, grad_mixed, preferred_element_type=jnp...  23.8 us
  transfers between devices with their start and end apart: 7, of which 7 were waited for; matrix products, arithmetic and copies ran while one was open for 2% of the time, Pallas kernels for 0%

profile of v1, /device:TPU:2, one launch (start us, length us, event | category | flops | bytes accessed | tf_op | source)
XLA Modules:
  0.0 1057.5 jit_solution(11824711245378906094)
XLA Ops:
  7.2 0.0 copy-start
  7.2 0.0 reduce-scatter.5.cloned.1.call-start
  7.2 0.9 copy-done
  8.1 2.3 fusion.39
  10.4 0.0 reduce-scatter.5.cloned.1.call-update
  10.5 0.0 all-gather.2.cloned.1.call-start
  10.5 30.2 %reduce-scatter.5.cloned.1.call-done = f32[64,512]{1,0:T(8,128)} async-done(((f32[256,512]{1,0:T(8,128)}), f32[64,512]{1,0:T(8,128)}) %reduce-scatter.5.cloned.1.call-update) | async-done | bytes 131088 | tf_op jit(solution)/shard_map/reduce_scatter | solution.py:46
  40.7 0.0 all-gather.2.cloned.1.call-update
  40.7 0.0 reduce-scatter.7.cloned.1.call-start
  41.4 0.7 compare_select_fusion.2
  42.1 0.0 copy-start.5
  42.1 14.1 %gather_fusion = f32[160,128,128]{2,1,0:T(8,128)} fusion(f32[160,128,128]{2,1,0:T(8,128)} %param.15, s32[1024]{0:T(1024)S(1)} %pad_clamp_fusion.2), kind=kCustom, calls=%fused_computation.clone | custom fusion | bytes 20972160 | tf_op jit(solution)/shard_map/jit(_take)/gather | solution.py:12
  56.3 0.0 copy-done.3
  56.3 0.0 copy-done.5
  56.3 10.5 all-gather.2.cloned.1.call-done
  66.9 1.3 copy_bitcast_fusion.2
  68.2 3.3 gather_fusion.1
  71.5 24.3 %fusion.20 = f32[64,160,128]{2,0,1:T(8,128)S(1)} fusion(f32[160,64,128]{2,1,0:T(8,128)} %gather_fusion.1, pred[160]{0:T(512)(128)(4,1)S(1)} %get-tuple-element.7, f32[160,128,128]{2,1,0:T(8,128)} %gather_fusion, pred[160]{0:T(512)(128)(4,1)S(1)} %get-tuple-element.8), kind=kOutput, calls=%fused_computation.23 | convolution fusion | flops 2017198080 | bytes 20971840 | tf_op jit(solution)/shard_map/fgb,gab->fga/dot_general | solution.py:16
  95.8 0.0 copy-start.2
  95.8 5.6 fusion.8
  101.4 1.6 copy.29
  103.0 0.0 reduce-scatter.7.cloned.1.call-update
  103.1 87.3 %reduce-scatter.7.cloned.1.call-done = f32[64,512]{1,0:T(8,128)} async-done(((f32[64,4096]{1,0:T(8,128)}), f32[64,512]{1,0:T(8,128)}) %reduce-scatter.7.cloned.1.call-update) | async-done | bytes 131088 | tf_op jit(solution)/shard_map/reduce_scatter | solution.py:62
  190.4 1.7 fusion.36
  192.0 1.1 stack.2
  193.1 4.5 all-to-all-start
  197.6 0.0 reduce-scatter.9.cloned.1.call-start
  197.7 27.0 %all-to-all-done = f32[8,64,512]{2,1,0:T(8,128)S(1)} async-done(((f32[8,64,512]{2,1,0:T(8,128)}), f32[8,64,512]{2,1,0:T(8,128)S(1)}, u32[]{:S(2)}, u32[]{:S(2)}) %all-to-all-start) | async-done | bytes 1048608 | tf_op jit(solution)/shard_map/all_to_all | solution.py:66
  224.6 0.6 copy.15
  225.2 0.1 reshape_reshape.3
  225.3 0.6 copy.16
  225.9 3.3 gather_fusion.2
  229.2 13.9 %fusion.25 = f32[64,160,128]{2,0,1:T(8,128)S(1)} fusion(f32[160,64,128]{2,1,0:T(8,128)} %gather_fusion.2, pred[160]{0:T(512)(128)(4,1)S(1)} %compare_and_fusion, f32[160,128,128]{2,1,0:T(8,128)} %gather_fusion, pred[160]{0:T(512)(128)(4,1)S(1)} %get-tuple-element.8), kind=kOutput, calls=%fused_computation.24 | convolution fusion | flops 2017198080 | bytes 20971840 | tf_op jit(solution)/shard_map/fga,gab->fgb/dot_general | solution.py:14
  243.1 0.0 copy-start.1
  243.1 5.6 fusion.6
  248.7 1.6 copy.28
  250.3 0.0 reduce-scatter.9.cloned.1.call-update
  250.3 0.0 all-reduce.2.cloned.1.call-start
  250.4 32.7 %reduce-scatter.9.cloned.1.call-done = f32[64,512]{1,0:T(8,128)} async-done(((f32[64,4096]{1,0:T(8,128)}), f32[64,512]{1,0:T(8,128)}) %reduce-scatter.9.cloned.1.call-update) | async-done | bytes 131088 | tf_op jit(solution)/shard_map/reduce_scatter | solution.py:71
  283.0 16.4 %all_gather.7 = f32[256,512]{1,0:T(8,128)S(1)} all-gather(f32[64,512]{1,0:T(8,128)} %reduce-scatter.9.cloned.1.call-done), channel_id=1, replica_groups=mesh['row'=8,'col'=8,'rep'=4] {'rep'}, dimensions={0}, use_global_device_ids=true | all-gather | bytes 655360 | tf_op jit(solution)/shard_map/all_gather | solution.py:85
  299.4 1.2 fusion.30
  300.7 0.0 all-reduce.2.cloned.1.call-update
  300.7 0.0 reduce-scatter.11.cloned.1.call-start
  300.7 2.3 fusion.37
  303.1 0.0 reduce-scatter.11.cloned.1.call-update
  303.1 722.3 %all-reduce.2.cloned.1.call-done = f32[64,256]{1,0:T(8,128)} async-done(((f32[64,256]{1,0:T(8,128)}), f32[64,256]{1,0:T(8,128)}) %all-reduce.2.cloned.1.call-update) | async-done | bytes 65552 | tf_op jit(solution)/shard_map/psum | solution.py:91
  1025.4 23.8 %reduce-scatter.11.cloned.1.call-done = f32[64,512]{1,0:T(8,128)} async-done(((f32[256,512]{1,0:T(8,128)}), f32[64,512]{1,0:T(8,128)}) %reduce-scatter.11.cloned.1.call-update) | async-done | bytes 131088 | tf_op jit(solution)/shard_map/reduce_scatter | solution.py:72
  1049.1 1.5 copy.32
  (13 shorter events, 0.1 us)
Async XLA Ops:
  7.2 1.0 copy-start
  7.2 33.5 %reduce-scatter.5.cloned.1.call-start = ((), (), s32[]{:S(2)}) async-start(), calls=%async_computation.5 | async-start | bytes 655360 | tf_op jit(solution)/shard_map/reduce_scatter | solution.py:46
  10.5 56.4 %all-gather.2.cloned.1.call-start = ((), (), s32[]{:S(2)}) async-start(), calls=%async_computation.6 | async-start | bytes 1179648 | tf_op jit(solution)/shard_map/all_gather | solution.py:58
  40.7 149.6 %reduce-scatter.7.cloned.1.call-start = ((), (), s32[]{:S(2)}) async-start(), calls=%async_computation.7 | async-start | bytes 1179648 | tf_op jit(solution)/shard_map/reduce_scatter | solution.py:62
  42.1 14.2 %copy-start.3 = (s32[160]{0:T(256)S(1)}, s32[160]{0:T(256)}, u32[]{:S(2)}) copy-start(s32[160]{0:T(256)} %param.17) | copy-start | bytes 1924
  42.1 14.2 %copy-start.5 = (s32[160]{0:T(256)S(1)}, s32[160]{0:T(256)}, u32[]{:S(2)}) copy-start(s32[160]{0:T(256)} %param.18) | copy-start | bytes 1924
  71.5 24.3 %copy-start.4 = (s32[160]{0:T(256)S(1)}, s32[160]{0:T(256)}, u32[]{:S(2)}) copy-start(s32[160]{0:T(256)} %param.16) | copy-start | bytes 1924
  95.8 94.6 %copy-start.2 = (f32[64,512]{1,0:T(8,128)S(1)}, f32[64,512]{1,0:T(8,128)}, u32[]{:S(2)}) copy-start(f32[64,512]{1,0:T(8,128)} %param.14) | copy-start | bytes 393220
  193.1 31.5 %all-to-all-start = ((f32[8,64,512]{2,1,0:T(8,128)}), f32[8,64,512]{2,1,0:T(8,128)S(1)}, u32[]{:S(2)}, u32[]{:S(2)}) async-start(f32[8,64,512]{2,1,0:T(8,128)} %stack.2), calls=%async_computation.2 | async-start | bytes 2097152 | tf_op jit(solution)/shard_map/all_to_all | solution.py:66
  197.6 85.4 %reduce-scatter.9.cloned.1.call-start = ((), (), s32[]{:S(2)}) async-start(), calls=%async_computation.8 | async-start | bytes 1179648 | tf_op jit(solution)/shard_map/reduce_scatter | solution.py:71
  243.1 56.4 %copy-start.1 = (f32[64,512]{1,0:T(8,128)S(1)}, f32[64,512]{1,0:T(8,128)}, u32[]{:S(2)}) copy-start(f32[64,512]{1,0:T(8,128)} %param.12) | copy-start | bytes 393220
  250.3 775.1 %all-reduce.2.cloned.1.call-start = ((), (), s32[]{:S(2)}) async-start(), calls=%async_computation.10 | async-start | bytes 131072 | tf_op jit(solution)/shard_map/psum | solution.py:91
  300.7 748.4 %reduce-scatter.11.cloned.1.call-start = ((), (), s32[]{:S(2)}) async-start(), calls=%async_computation.9 | async-start | bytes 655360 | tf_op jit(solution)/shard_map/reduce_scatter | solution.py:72
Sparse Core Ops, SparseCore 0:
  10.6 30.0 reduce-scatter.4
  42.5 24.2 all-gather.1
  103.2 87.1 reduce-scatter.6
  250.4 32.5 reduce-scatter.8
  300.8 724.5 all-reduce.1
  1028.3 20.7 reduce-scatter.10
